TPU v7x, 32 devices: a whole 2x2x4 slice. The times are simulated.
32 devices in a mesh: ctx: 8 (over z, y), fsdp: 4 (over x, core).
Axes of the slice: x: 2, y: 2, z: 4, core: 2. Of those that a mesh axis runs over, the one named last changes fastest.
Arguments:
- tokens: bfloat16 [4, 2048, 1024], P('fsdp', 'ctx'), may hold values from -6 to 6
- out_grad: bfloat16 [4, 2048, 1024], P('fsdp', 'ctx'), may hold values from -6 to 6
- lengths: int32 [4, 1], P('fsdp'), may hold values from 512 to 2048, as said below
- norm1_gain: bfloat16 [1024], P('fsdp'), may hold values from 0.5 to 1.5
- w_query: bfloat16 [1024, 1024], P('fsdp'), may hold values from -0.1875 to 0.1875
- w_latent: bfloat16 [1024, 512], P('fsdp'), may hold values from -0.1875 to 0.1875
- w_key_up: bfloat16 [1024, 256], P('fsdp'), may hold values from -0.75 to 0.75
- w_value_up: bfloat16 [1024, 256], P('fsdp'), may hold values from -0.375 to 0.375
- w_output: bfloat16 [1024, 1024], P('fsdp'), may hold values from -1.5 to 1.5
- norm2_gain: bfloat16 [1024], P('fsdp'), may hold values from 0.5 to 1.5
- w_gate: bfloat16 [1024, 2816], P(None, 'fsdp'), may hold values from -0.1875 to 0.1875
- w_up: bfloat16 [1024, 2816], P(None, 'fsdp'), may hold values from -0.1875 to 0.1875
- w_down: bfloat16 [2816, 1024], P('fsdp'), may hold values from -0.109375 to 0.109375
Outputs:
- result: bfloat16 [4, 2048, 1024], P('fsdp', 'ctx')
- token_grad: float32 [4, 2048, 1024], P('fsdp', 'ctx')
- norm1_gain_grad: float32 [1024], P('fsdp')
- w_query_grad: float32 [1024, 1024], P('fsdp')
- w_latent_grad: float32 [1024, 512], P('fsdp')
- w_key_up_grad: float32 [1024, 256], P('fsdp')
- w_value_up_grad: float32 [1024, 256], P('fsdp')
- w_output_grad: float32 [1024, 1024], P('fsdp')
- norm2_gain_grad: float32 [1024], P('fsdp')
- w_gate_grad: float32 [1024, 2816], P(None, 'fsdp')
- w_up_grad: float32 [1024, 2816], P(None, 'fsdp')
- w_down_grad: float32 [2816, 1024], P('fsdp')
Inputs may be any that keep to these rules, and one draw needn't show every extreme that they name: lengths[g, j] valid tokens stand at the start of slot j of group g; the rest of the slot of 2048 rows is padding.
All inputs are finite; a program needn't handle non-finite values.
Results may differ from a plain program's by a relative error of at most 0.025.
Values may be sent and summed in bfloat16 or wider, within the bound.
No kernel may reach another device: no remote copies, remote signals or barrier semaphores. Data moves between devices by JAX's collectives and lax.ppermute only.
A program may use at most 192 MiB of HBM per device.

v0:
```python
import jax
import jax.numpy as jnp
from jax import lax
from jax.sharding import PartitionSpec as P

NH = 16
HD = 64
LAT = 256
GRP = 2
SEQ_MAX = 4096
EPS = 1e-06
NEGATIVE = -1e30


def norm_scale(values):
    return lax.rsqrt(jnp.mean(values * values, axis=-1, keepdims=True) + EPS)


def norm_back(grad_in, normed, scale_rows, gain_full):
    scaled = grad_in * gain_full
    return scale_rows * (scaled - normed * jnp.mean(scaled * normed, axis=-1, keepdims=True))


def key_mask(key_start, key_rows, slot_start, query_pos, length):
    relative = key_start - slot_start + jnp.arange(key_rows, dtype=jnp.int32)
    return (
        (relative[None, :] >= 0)
        & (relative[None, :] <= query_pos[:, None])
        & (relative[None, :] < length)
    )


def raw_scores(query_groups, key_piece, allowed, score_scale):
    grouped = key_piece.reshape(key_piece.shape[0], GRP, LAT)
    scores = (
        jnp.einsum("gpql,kgl->gpqk", query_groups, grouped, preferred_element_type=jnp.float32)
        * score_scale
    )
    return (jnp.where(allowed[None, None], scores, NEGATIVE), grouped)


def on_device(
    tokens,
    out_grad,
    lengths,
    norm1_gain,
    w_query,
    w_latent,
    w_key_up,
    w_value_up,
    w_output,
    norm2_gain,
    w_gate,
    w_up,
    w_down,
):
    ctx_size = lax.axis_size("ctx")
    tok_rows = tokens.shape[1]
    group_rows = tok_rows * ctx_size
    seq_rows = min(SEQ_MAX, group_rows)
    slot_blocks = seq_rows // tok_rows
    head_groups = NH // GRP
    lat_width = GRP * LAT
    my_start = lax.axis_index("ctx") * tok_rows
    slot_number = my_start // seq_rows
    slot_start = slot_number * seq_rows
    length = jnp.sum(
        jnp.where(jnp.arange(lengths.shape[1], dtype=jnp.int32) == slot_number, lengths[0], 0)
    )
    query_pos = my_start - slot_start + jnp.arange(tok_rows, dtype=jnp.int32)
    row_valid = (query_pos < length).astype(jnp.float32)[:, None]
    score_scale = HD ** (-0.5)
    gain_one, query_full, latent_full, key_full, value_full, output_full = (
        lax.all_gather(norm1_gain, "fsdp", axis=0, tiled=True),
        lax.all_gather(w_query, "fsdp", axis=0, tiled=True),
        lax.all_gather(w_latent, "fsdp", axis=0, tiled=True),
        lax.all_gather(w_key_up, "fsdp", axis=0, tiled=True),
        lax.all_gather(w_value_up, "fsdp", axis=0, tiled=True),
        lax.all_gather(w_output, "fsdp", axis=0, tiled=True),
    )
    gain_two, gate_full, up_full, down_full = (
        lax.all_gather(norm2_gain, "fsdp", axis=0, tiled=True),
        lax.all_gather(w_gate, "fsdp", axis=1, tiled=True),
        lax.all_gather(w_up, "fsdp", axis=1, tiled=True),
        lax.all_gather(w_down, "fsdp", axis=0, tiled=True),
    )
    gain_one_f = gain_one.astype(jnp.float32)
    gain_two_f = gain_two.astype(jnp.float32)
    inputs = tokens[0].astype(jnp.float32)
    scale_one = norm_scale(inputs)
    normed_one = inputs * scale_one
    normed = (normed_one * gain_one_f).astype(jnp.bfloat16)
    queries = jnp.dot(normed, query_full, preferred_element_type=jnp.float32).astype(jnp.bfloat16)
    latent = jnp.dot(normed, latent_full, preferred_element_type=jnp.float32).astype(jnp.bfloat16)
    key_heads = key_full.reshape(NH, HD, LAT)
    query_latent = jnp.einsum(
        "shd,hdl->hsl",
        queries.reshape(tok_rows, NH, HD),
        key_heads,
        preferred_element_type=jnp.float32,
    ).astype(jnp.bfloat16)
    query_groups = query_latent.reshape(GRP, head_groups, tok_rows, LAT)

    def is_needed(key_start, key_rows):
        return (
            (key_start + key_rows > slot_start)
            & (key_start < slot_start + length)
            & (key_start < my_start + tok_rows)
        )

    def forward_update(state_now, key_piece, key_start):
        best_now, weight_sum, accum_now = state_now
        allowed = key_mask(key_start, key_piece.shape[0], slot_start, query_pos, length)
        scores, grouped = raw_scores(query_groups, key_piece, allowed, score_scale)
        best_next = jnp.maximum(best_now, jnp.max(scores, axis=-1))
        factor = jnp.exp(best_now - best_next)
        weights = jnp.where(allowed[None, None], jnp.exp(scores - best_next[..., None]), 0.0)
        weight_sum = weight_sum * factor + jnp.sum(weights, axis=-1)
        accum_now = accum_now * factor[..., None] + jnp.einsum(
            "gpqk,kgl->gpql",
            weights.astype(jnp.bfloat16),
            grouped,
            preferred_element_type=jnp.float32,
        )
        return (best_next, weight_sum, accum_now)

    def guarded_forward(state_now, key_piece, key_start):
        return lax.cond(
            is_needed(key_start, key_piece.shape[0]),
            lambda state_in: forward_update(state_in, key_piece, key_start),
            lambda state_in: state_in,
            state_now,
        )

    start_state = (
        jnp.full((GRP, head_groups, tok_rows), NEGATIVE, jnp.float32),
        jnp.zeros((GRP, head_groups, tok_rows), jnp.float32),
        jnp.zeros((GRP, head_groups, tok_rows, LAT), jnp.float32),
    )
    group_latent = lax.all_gather(latent, "ctx", axis=0, tiled=True)

    def forward_loop(block_index, state_now):
        key_start = slot_start + block_index * tok_rows
        key_piece = lax.dynamic_slice_in_dim(group_latent, key_start, tok_rows, 0)
        return guarded_forward(state_now, key_piece, key_start)

    final_state = lax.fori_loop(0, slot_blocks, forward_loop, start_state)
    best_final, sum_final, accum_final = final_state
    log_total = best_final + jnp.log(sum_final)
    mixture = accum_final / sum_final[..., None]
    mixture_low = mixture.astype(jnp.bfloat16)
    value_heads = value_full.reshape(NH, HD, LAT)
    attended = (
        jnp.einsum(
            "hsl,hdl->shd",
            mixture_low.reshape(NH, tok_rows, LAT),
            value_heads,
            preferred_element_type=jnp.float32,
        )
        .reshape(tok_rows, NH * HD)
        .astype(jnp.bfloat16)
    )
    branch = jnp.dot(attended, output_full, preferred_element_type=jnp.float32)
    middle = inputs + branch
    scale_two = norm_scale(middle)
    normed_two_raw = middle * scale_two
    normed_two = (normed_two_raw * gain_two_f).astype(jnp.bfloat16)
    gate_value = jnp.dot(normed_two, gate_full, preferred_element_type=jnp.float32)
    upward = jnp.dot(normed_two, up_full, preferred_element_type=jnp.float32)
    sigmoid_gate = jax.nn.sigmoid(gate_value)
    silu_gate = gate_value * sigmoid_gate
    hidden = (silu_gate * upward).astype(jnp.bfloat16)
    feed_out = jnp.dot(hidden, down_full, preferred_element_type=jnp.float32)
    result = ((middle + feed_out) * row_valid).astype(jnp.bfloat16)
    cotangent = out_grad[0].astype(jnp.float32) * row_valid
    feed_grad = cotangent.astype(jnp.bfloat16)
    down_grad = jnp.einsum("tf,td->fd", hidden, feed_grad, preferred_element_type=jnp.float32)
    hidden_grad = jnp.einsum("td,fd->tf", feed_grad, down_full, preferred_element_type=jnp.float32)
    gate_grad = (
        hidden_grad * upward * sigmoid_gate * (1.0 + gate_value * (1.0 - sigmoid_gate))
    ).astype(jnp.bfloat16)
    up_grad_in = (hidden_grad * silu_gate).astype(jnp.bfloat16)
    gate_w_grad = jnp.einsum("td,tf->df", normed_two, gate_grad, preferred_element_type=jnp.float32)
    up_w_grad = jnp.einsum("td,tf->df", normed_two, up_grad_in, preferred_element_type=jnp.float32)
    normed_two_grad = jnp.einsum(
        "tf,df->td", gate_grad, gate_full, preferred_element_type=jnp.float32
    ) + jnp.einsum("tf,df->td", up_grad_in, up_full, preferred_element_type=jnp.float32)
    gain_two_grad = jnp.sum(normed_two_grad * normed_two_raw, axis=0)
    middle_grad = cotangent + norm_back(normed_two_grad, normed_two_raw, scale_two, gain_two_f)
    branch_grad = middle_grad.astype(jnp.bfloat16)
    output_grad = jnp.einsum("tk,td->kd", attended, branch_grad, preferred_element_type=jnp.float32)
    attended_grad = jnp.einsum(
        "td,kd->tk", branch_grad, output_full, preferred_element_type=jnp.float32
    ).astype(jnp.bfloat16)
    attended_heads = attended_grad.reshape(tok_rows, NH, HD)
    value_grad = jnp.einsum(
        "shd,hsl->hdl",
        attended_heads,
        mixture_low.reshape(NH, tok_rows, LAT),
        preferred_element_type=jnp.float32,
    ).reshape(NH * HD, LAT)
    mixture_grad = (
        jnp.einsum("shd,hdl->hsl", attended_heads, value_heads, preferred_element_type=jnp.float32)
        .astype(jnp.bfloat16)
        .reshape(GRP, head_groups, tok_rows, LAT)
    )
    delta_sum = jnp.sum(mixture_grad * mixture, axis=-1)

    def back_term(query_grad_sum, key_piece, key_start):

        def compute(sum_in):
            allowed = key_mask(key_start, tok_rows, slot_start, query_pos, length)
            scores, grouped = raw_scores(query_groups, key_piece, allowed, score_scale)
            probs = jnp.where(allowed[None, None], jnp.exp(scores - log_total[..., None]), 0.0)
            probs_low = probs.astype(jnp.bfloat16)
            prob_grad = jnp.einsum(
                "gpql,kgl->gpqk", mixture_grad, grouped, preferred_element_type=jnp.float32
            )
            score_grad = (probs * (prob_grad - delta_sum[..., None])).astype(jnp.bfloat16)
            sum_out = sum_in + score_scale * jnp.einsum(
                "gpqk,kgl->gpql", score_grad, grouped, preferred_element_type=jnp.float32
            )
            key_term = score_scale * jnp.einsum(
                "gpqk,gpql->kgl", score_grad, query_groups, preferred_element_type=jnp.float32
            ) + jnp.einsum(
                "gpqk,gpql->kgl", probs_low, mixture_grad, preferred_element_type=jnp.float32
            )
            return (sum_out, key_term.reshape(tok_rows, lat_width))

        def skipped(sum_in):
            return (sum_in, jnp.zeros((tok_rows, lat_width), jnp.float32))

        return lax.cond(is_needed(key_start, tok_rows), compute, skipped, query_grad_sum)

    zero_query = jnp.zeros((GRP, head_groups, tok_rows, LAT), jnp.float32)

    def backward_loop(block_index, state_now):
        sum_now, key_grads = state_now
        key_start = slot_start + block_index * tok_rows
        key_piece = lax.dynamic_slice_in_dim(group_latent, key_start, tok_rows, 0)
        sum_now, key_term = back_term(sum_now, key_piece, key_start)
        key_grads = lax.dynamic_update_slice_in_dim(key_grads, key_term, block_index * tok_rows, 0)
        return (sum_now, key_grads)

    back_start = (zero_query, jnp.zeros((seq_rows, lat_width), jnp.float32))
    query_lat_grad, slot_key_grads = lax.fori_loop(0, slot_blocks, backward_loop, back_start)
    row_count = tok_rows * lax.axis_size("ctx")
    padding = jnp.zeros((row_count, lat_width), jnp.float32)
    padded = jnp.concatenate([padding, slot_key_grads, padding], axis=0)
    offset = jnp.clip(jnp.int32(0) - slot_start + row_count, 0, seq_rows + row_count)
    latent_grad = lax.psum_scatter(
        lax.dynamic_slice_in_dim(padded, offset, row_count, 0).astype(jnp.bfloat16),
        "ctx",
        scatter_dimension=0,
        tiled=True,
    )
    query_lat_low = query_lat_grad.reshape(NH, tok_rows, LAT).astype(jnp.bfloat16)
    key_up_grad = jnp.einsum(
        "shd,hsl->hdl",
        queries.reshape(tok_rows, NH, HD),
        query_lat_low,
        preferred_element_type=jnp.float32,
    ).reshape(NH * HD, LAT)
    query_grad = (
        jnp.einsum("hsl,hdl->shd", query_lat_low, key_heads, preferred_element_type=jnp.float32)
        .reshape(tok_rows, NH * HD)
        .astype(jnp.bfloat16)
    )
    query_w_grad = jnp.einsum("td,tk->dk", normed, query_grad, preferred_element_type=jnp.float32)
    latent_w_grad = jnp.einsum("td,tk->dk", normed, latent_grad, preferred_element_type=jnp.float32)
    normed_grad = jnp.einsum(
        "tk,dk->td", query_grad, query_full, preferred_element_type=jnp.float32
    ) + jnp.einsum("tk,dk->td", latent_grad, latent_full, preferred_element_type=jnp.float32)
    gain_one_grad = jnp.sum(normed_grad * normed_one, axis=0)
    input_grad = middle_grad + norm_back(normed_grad, normed_one, scale_one, gain_one_f)
    shards = (
        lax.psum_scatter(
            gain_one_grad.astype(jnp.bfloat16), "fsdp", scatter_dimension=0, tiled=True
        ).astype(jnp.float32),
        lax.psum_scatter(
            query_w_grad.astype(jnp.bfloat16), "fsdp", scatter_dimension=0, tiled=True
        ).astype(jnp.float32),
        lax.psum_scatter(
            latent_w_grad.astype(jnp.bfloat16), "fsdp", scatter_dimension=0, tiled=True
        ).astype(jnp.float32),
        lax.psum_scatter(
            key_up_grad.astype(jnp.bfloat16), "fsdp", scatter_dimension=0, tiled=True
        ).astype(jnp.float32),
        lax.psum_scatter(
            value_grad.astype(jnp.bfloat16), "fsdp", scatter_dimension=0, tiled=True
        ).astype(jnp.float32),
        lax.psum_scatter(
            output_grad.astype(jnp.bfloat16), "fsdp", scatter_dimension=0, tiled=True
        ).astype(jnp.float32),
        lax.psum_scatter(
            gain_two_grad.astype(jnp.bfloat16), "fsdp", scatter_dimension=0, tiled=True
        ).astype(jnp.float32),
        lax.psum_scatter(
            gate_w_grad.astype(jnp.bfloat16), "fsdp", scatter_dimension=1, tiled=True
        ).astype(jnp.float32),
        lax.psum_scatter(
            up_w_grad.astype(jnp.bfloat16), "fsdp", scatter_dimension=1, tiled=True
        ).astype(jnp.float32),
        lax.psum_scatter(
            down_grad.astype(jnp.bfloat16), "fsdp", scatter_dimension=0, tiled=True
        ).astype(jnp.float32),
    )
    summed = (
        lax.psum(shards[0].astype(jnp.bfloat16), "ctx").astype(jnp.float32),
        lax.psum(shards[1].astype(jnp.bfloat16), "ctx").astype(jnp.float32),
        lax.psum(shards[2].astype(jnp.bfloat16), "ctx").astype(jnp.float32),
        lax.psum(shards[3].astype(jnp.bfloat16), "ctx").astype(jnp.float32),
        lax.psum(shards[4].astype(jnp.bfloat16), "ctx").astype(jnp.float32),
        lax.psum(shards[5].astype(jnp.bfloat16), "ctx").astype(jnp.float32),
        lax.psum(shards[6].astype(jnp.bfloat16), "ctx").astype(jnp.float32),
        lax.psum(shards[7].astype(jnp.bfloat16), "ctx").astype(jnp.float32),
        lax.psum(shards[8].astype(jnp.bfloat16), "ctx").astype(jnp.float32),
        lax.psum(shards[9].astype(jnp.bfloat16), "ctx").astype(jnp.float32),
    )
    return (
        result[None],
        input_grad[None],
        summed[0],
        summed[1],
        summed[2],
        summed[3],
        summed[4],
        summed[5],
        summed[6],
        summed[7],
        summed[8],
        summed[9],
    )


def solution(mesh):
    return jax.shard_map(
        on_device,
        mesh=mesh,
        in_specs=(
            P("fsdp", "ctx", None),
            P("fsdp", "ctx", None),
            P("fsdp", None),
            P("fsdp"),
            P("fsdp", None),
            P("fsdp", None),
            P("fsdp", None),
            P("fsdp", None),
            P("fsdp", None),
            P("fsdp"),
            P(None, "fsdp"),
            P(None, "fsdp"),
            P("fsdp", None),
        ),
        out_specs=(
            P("fsdp", "ctx", None),
            P("fsdp", "ctx", None),
            P("fsdp"),
            P("fsdp", None),
            P("fsdp", None),
            P("fsdp", None),
            P("fsdp", None),
            P("fsdp", None),
            P("fsdp"),
            P(None, "fsdp"),
            P(None, "fsdp"),
            P("fsdp", None),
        ),
        check_vma=False,
    )
```

profile of v0, /device:TPU:0, one launch (start us, length us, event | category | flops | bytes accessed | tf_op | source)
XLA Modules:
  0.0 1036.9 jit_solution(728526672755502800)
XLA Ops:
  9.4 6.0 all-gather
  16.6 12.5 %all-gather.10.cloned.1.call-done = bf16[1024,512]{1,0:T(8,128)(2,1)} async-done(((bf16[256,512]{1,0:T(8,128)(2,1)}), bf16[1024,512]{1,0:T(8,128)(2,1)}) %all-gather.10.cloned.1.call-update) | async-done | bytes 1048592 | tf_op jit(solution)/shard_map/all_gather | solution.py:76
  40.0 10.9 %all_gather.38 = bf16[1024,256]{1,0:T(8,128)(2,1)} all-gather(bf16[256,256]{1,0:T(8,128)(2,1)S(1)} %copy-done.41), channel_id=1, replica_groups=mesh['ctx'=8,'fsdp'=4] {'fsdp'}, dimensions={0}, use_global_device_ids=true | all-gather | bytes 655360 | tf_op jit(solution)/shard_map/all_gather | solution.py:78
  50.9 7.3 all_gather.37
  65.9 42.2 %all-gather.12.cloned.1.call-done = bf16[2048,512]{1,0:T(8,128)(2,1)} async-done(((bf16[256,512]{1,0:T(8,128)(2,1)}), bf16[2048,512]{1,0:T(8,128)(2,1)}) %all-gather.12.cloned.1.call-update) | async-done | bytes 2097168 | tf_op jit(solution)/shard_map/all_gather | solution.py:140
  114.5 10.8 %while.41 = (s32[]{:T(128)}, f32[2,8,256]{2,1,0:T(8,128)S(1)}, f32[2,8,256]{2,1,0:T(8,128)S(1)}, f32[2,8,256,256]{3,2,1,0:T(8,128)}, s32[]{:T(128)}, /*index=5*/...) while((s32[]{:T(128)}, f32[2,8,256]{2,1,0:T(8,128)S(1)}, ...), condition=%wide.region_6.7_spmd.clone, body=%wide.region_1.6_spmd.clone.sunk | while | flops 1089676544 | bytes 58203600 | solution.py:147
  114.5 10.4 %conditional.6 = ((f32[2,8,256]{2,1,0:T(8,128)S(1)}, f32[2,8,256]{2,1,0:T(8,128)S(1)}, f32[2,8,256,256]{3,2,1,0:T(8,128)})) conditional(s32[]{:T(128)} %convert_element_type.380, (f32[2,8,256]{2,1,0:T(8,128)S(1)}, f32[2,8,256]{2,1,0:T(8,128)S(1)}, f32[2,8,256,256]{3,2,1,0:T(8,128)}) %tuple.129, (s32[]{:T(128)}, s32[]{:T(128)}, s32[]{:T(128)}, ...), branch_computations={%region_2.2_spmd, %region_3.5_spmd} | conditional | flops 1089676544 | bytes 58202268 | solution.py:128
  139.3 36.1 %all-gather.18.cloned.1.call-done = bf16[1024,2816]{0,1:T(8,128)(2,1)} async-done(((bf16[1024,704]{0,1:T(8,128)(2,1)}), bf16[1024,2816]{0,1:T(8,128)(2,1)}) %all-gather.18.cloned.1.call-update) | async-done | bytes 5767184 | tf_op jit(solution)/shard_map/all_gather | solution.py:83
  181.4 38.9 %all-gather.20.cloned.1.call-done = bf16[1024,2816]{0,1:T(8,128)(2,1)} async-done(((bf16[1024,704]{0,1:T(8,128)(2,1)}), bf16[1024,2816]{0,1:T(8,128)(2,1)}) %all-gather.20.cloned.1.call-update) | async-done | bytes 5767184 | tf_op jit(solution)/shard_map/all_gather | solution.py:84
  226.2 39.1 %all-gather.22.cloned.1.call-done = bf16[2816,1024]{1,0:T(8,128)(2,1)} async-done(((bf16[704,1024]{1,0:T(8,128)(2,1)}), bf16[2816,1024]{1,0:T(8,128)(2,1)}) %all-gather.22.cloned.1.call-update) | async-done | bytes 5767184 | tf_op jit(solution)/shard_map/all_gather | solution.py:85
  265.3 8.2 multiply_convert_fusion
  296.3 20.4 %while.42 = (s32[]{:T(128)}, f32[2,8,256,256]{3,2,1,0:T(8,128)}, bf16[2048,512]{0,1:T(8,128)(2,1)}, s32[]{:T(128)}, s32[]{:T(128)}, /*index=5*/s32[]{:T(128)}, s...) while((s32[]{:T(128)}, f32[2,8,256,256]{3,2,1,0:T(8,128)}, ...), condition=%wide.region_13.14_spmd.clone, body=%wide.region_10.13_spmd.clone.sunk | while | flops 2699625728 | bytes 97771040 | solution.py:246
  296.3 14.2 %conditional.7 = (f32[2,8,256,256]{3,2,1,0:T(8,128)}, bf16[256,512]{0,1:T(8,128)(2,1)S(1)}) conditional(s32[]{:T(128)} %convert_element_type.381, f32[2,8,256,256]{3,2,1,0:T(8,128)} %get-tuple-element.1157, (s32[]{:T(128)}, s32[]{:T(128)}, s32[]{:T(128)}, s32[]{:T(128)}, bf16[2048,512]{0,1:T(8,128)(2,1)}, ...), branch_computations={%region_11.11_spmd, %region_12.12_spmd} | conditional | flops 2699625728 | bytes 97245368 | solution.py:233
  337.6 152.6 %reduce-scatter.10.cloned.1.call-done = bf16[256,512]{0,1:T(8,128)(2,1)} async-done(((bf16[2048,512]{0,1:T(8,128)(2,1)}), bf16[256,512]{0,1:T(8,128)(2,1)}) %reduce-scatter.10.cloned.1.call-update) | async-done | bytes 262160 | tf_op jit(solution)/shard_map/reduce_scatter | solution.py:251
  513.4 24.2 %reduce-scatter.18.cloned.1.call-done = bf16[256,256]{1,0:T(8,128)(2,1)} async-done(((bf16[1024,256]{1,0:T(8,128)(2,1)}), bf16[256,256]{1,0:T(8,128)(2,1)}) %reduce-scatter.18.cloned.1.call-update) | async-done | bytes 131088 | tf_op jit(solution)/shard_map/reduce_scatter | solution.py:289
  537.6 34.6 %reduce-scatter.12.cloned.1.call-done = bf16[256,1024]{1,0:T(8,128)(2,1)} async-done(((bf16[1024,1024]{1,0:T(8,128)(2,1)}), bf16[256,1024]{1,0:T(8,128)(2,1)}) %reduce-scatter.12.cloned.1.call-update) | async-done | bytes 524304 | tf_op jit(solution)/shard_map/reduce_scatter | solution.py:280
  572.2 34.6 %reduce-scatter.20.cloned.1.call-done = bf16[256,1024]{1,0:T(8,128)(2,1)} async-done(((bf16[1024,1024]{1,0:T(8,128)(2,1)}), bf16[256,1024]{1,0:T(8,128)(2,1)}) %reduce-scatter.20.cloned.1.call-update) | async-done | bytes 524304 | tf_op jit(solution)/shard_map/reduce_scatter | solution.py:292
  606.8 28.0 %reduce-scatter.14.cloned.1.call-done = bf16[256,512]{1,0:T(8,128)(2,1)} async-done(((bf16[1024,512]{1,0:T(8,128)(2,1)}), bf16[256,512]{1,0:T(8,128)(2,1)}) %reduce-scatter.14.cloned.1.call-update) | async-done | bytes 262160 | tf_op jit(solution)/shard_map/reduce_scatter | solution.py:283
  634.8 57.5 %reduce-scatter.22.cloned.1.call-done = bf16[1024,704]{0,1:T(8,128)(2,1)} async-done(((bf16[1024,2816]{0,1:T(8,128)(2,1)}), bf16[1024,704]{0,1:T(8,128)(2,1)}) %reduce-scatter.22.cloned.1.call-update) | async-done | bytes 1441808 | tf_op jit(solution)/shard_map/reduce_scatter | solution.py:298
  692.3 57.3 %reduce-scatter.24.cloned.1.call-done = bf16[1024,704]{0,1:T(8,128)(2,1)} async-done(((bf16[1024,2816]{0,1:T(8,128)(2,1)}), bf16[1024,704]{0,1:T(8,128)(2,1)}) %reduce-scatter.24.cloned.1.call-update) | async-done | bytes 1441808 | tf_op jit(solution)/shard_map/reduce_scatter | solution.py:301
  749.6 57.5 %reduce-scatter.26.cloned.1.call-done = bf16[704,1024]{1,0:T(8,128)(2,1)} async-done(((bf16[2816,1024]{1,0:T(8,128)(2,1)}), bf16[704,1024]{1,0:T(8,128)(2,1)}) %reduce-scatter.26.cloned.1.call-update) | async-done | bytes 1441808 | tf_op jit(solution)/shard_map/reduce_scatter | solution.py:304
  817.5 6.1 all-reduce.4
  823.7 22.1 %all-reduce.2 = (bf16[256]{0:T(256)(128)(2,1)S(1)}, bf16[256]{0:T(256)(128)(2,1)S(1)}) all-reduce(bf16[256]{0:T(256)(128)(2,1)S(1)} %dynamic-slice.1, bf16[256]{0:T(256)(128)(2,1)S(1)} %dynamic-slice.3), channel_id=1, replica_groups=mesh['ctx'=8,'fsdp'=4] {'ctx'}, use_global_device_ids=true, to_apply=%region_18.19 | all-reduce | flops 512 | bytes 2048 | tf_op jit(solution)/shard_map/psum | solution.py:309
  848.2 167.7 %all-reduce.7.cloned.1.call-done = (bf16[256,1024]{1,0:T(8,128)(2,1)}, bf16[256,512]{1,0:T(8,128)(2,1)}, bf16[256,256]{1,0:T(8,128)(2,1)}, bf16[256,256]{1,0:T(8...) async-done(((bf16[256,1024]{1,0:T(8,128)(2,1)}, bf16[256,512]{1,0:T(8,128)(2,1)}, ...) | async-done | bytes 5898256 | tf_op jit(solution)/shard_map/psum | solution.py:310
  (259 shorter events, 177.2 us)
Async XLA Ops:
  7.2 21.8 %all-gather.10.cloned.1.call-start = ((), (), s32[]{:S(2)}) async-start(), calls=%async_computation.9 | async-start | bytes 1310720 | tf_op jit(solution)/shard_map/all_gather | solution.py:76
  7.9 50.3 %all-gather.14.cloned.1.call-start = ((), (), s32[]{:S(2)}) async-start(), calls=%async_computation.11 | async-start | bytes 2621440 | tf_op jit(solution)/shard_map/all_gather | solution.py:75
  8.7 99.4 %all-gather.12.cloned.1.call-start = ((), (), s32[]{:S(2)}) async-start(), calls=%async_computation.10 | async-start | bytes 2359296 | tf_op jit(solution)/shard_map/all_gather | solution.py:140
  31.6 8.4 copy-start.41
  31.6 19.3 %copy-start.42 = (bf16[256,256]{1,0:T(8,128)(2,1)S(1)}, bf16[256,256]{1,0:T(8,128)(2,1)}, u32[]{:S(2)}) copy-start(bf16[256,256]{1,0:T(8,128)(2,1)} %param.27) | copy-start | bytes 393220
  31.6 104.0 %all-gather.16.cloned.1.call-start = ((), (), s32[]{:S(2)}) async-start(), calls=%async_computation.12 | async-start | bytes 2621440 | tf_op jit(solution)/shard_map/all_gather | solution.py:79
  32.2 26.0 %copy-start.8 = (bf16[1,256,1024]{2,1,0:T(8,128)(2,1)S(1)}, bf16[1,256,1024]{2,1,0:T(8,128)(2,1)}, u32[]{:S(2)}) copy-start(bf16[1,256,1024]{2,1,0:T(8,128)(2,1)} %param.21) | copy-start | bytes 1572868
  32.2 143.2 %all-gather.18.cloned.1.call-start = ((), (), s32[]{:S(2)}) async-start(), calls=%async_computation.13 | async-start | bytes 7208960 | tf_op jit(solution)/shard_map/all_gather | solution.py:83
  32.8 187.5 %all-gather.20.cloned.1.call-start = ((), (), s32[]{:S(2)}) async-start(), calls=%async_computation.14 | async-start | bytes 7208960 | tf_op jit(solution)/shard_map/all_gather | solution.py:84
  33.4 231.9 %all-gather.22.cloned.1.call-start = ((), (), s32[]{:S(2)}) async-start(), calls=%async_computation.15 | async-start | bytes 7208960 | tf_op jit(solution)/shard_map/all_gather | solution.py:85
  34.1 456.1 %reduce-scatter.10.cloned.1.call-start = ((), (), s32[]{:S(2)}) async-start(), calls=%async_computation.16 | async-start | bytes 2359296 | tf_op jit(solution)/shard_map/reduce_scatter | solution.py:251
  139.3 81.0 %copy-start.18 = (bf16[256,1024]{1,0:T(8,128)(2,1)}, bf16[256,1024]{1,0:T(8,128)(2,1)S(1)}, u32[]{:S(2)}) copy-start(bf16[256,1024]{1,0:T(8,128)(2,1)S(1)} %multiply_convert_fusion.3) | copy-start | bytes 1572868
  322.6 190.8 %reduce-scatter.16.cloned.1.call-start = ((), (), s32[]{:S(2)}) async-start(), calls=%async_computation.19 | async-start | bytes 655360 | tf_op jit(solution)/shard_map/reduce_scatter | solution.py:286
  327.8 209.8 %reduce-scatter.18.cloned.1.call-start = ((), (), s32[]{:S(2)}) async-start(), calls=%async_computation.20 | async-start | bytes 655360 | tf_op jit(solution)/shard_map/reduce_scatter | solution.py:289
  330.6 241.6 %reduce-scatter.12.cloned.1.call-start = ((), (), s32[]{:S(2)}) async-start(), calls=%async_computation.17 | async-start | bytes 2621440 | tf_op jit(solution)/shard_map/reduce_scatter | solution.py:280
  335.2 271.6 %reduce-scatter.20.cloned.1.call-start = ((), (), s32[]{:S(2)}) async-start(), calls=%async_computation.21 | async-start | bytes 2621440 | tf_op jit(solution)/shard_map/reduce_scatter | solution.py:292
  337.5 155.3 %copy-start.19 = (bf16[256,1024]{1,0:T(8,128)(2,1)S(1)}, bf16[256,1024]{1,0:T(8,128)(2,1)}, u32[]{:S(2)}) copy-start(bf16[256,1024]{1,0:T(8,128)(2,1)} %copy-done.18) | copy-start | bytes 1572868
  337.6 297.3 %reduce-scatter.14.cloned.1.call-start = ((), (), s32[]{:S(2)}) async-start(), calls=%async_computation.18 | async-start | bytes 1310720 | tf_op jit(solution)/shard_map/reduce_scatter | solution.py:283
  492.8 199.5 %reduce-scatter.22.cloned.1.call-start = ((), (), s32[]{:S(2)}) async-start(), calls=%async_computation.22 | async-start | bytes 7208960 | tf_op jit(solution)/shard_map/reduce_scatter | solution.py:298
  498.4 251.2 %reduce-scatter.24.cloned.1.call-start = ((), (), s32[]{:S(2)}) async-start(), calls=%async_computation.23 | async-start | bytes 7208960 | tf_op jit(solution)/shard_map/reduce_scatter | solution.py:301
  504.1 302.9 %reduce-scatter.26.cloned.1.call-start = ((), (), s32[]{:S(2)}) async-start(), calls=%async_computation.24 | async-start | bytes 7208960 | tf_op jit(solution)/shard_map/reduce_scatter | solution.py:304
  510.8 505.1 %all-reduce.7.cloned.1.call-start = ((), (), s32[]{:S(2)}) async-start(), calls=%async_computation.25 | async-start | bytes 11796480 | tf_op jit(solution)/shard_map/psum | solution.py:310
  1015.9 7.3 copy-start.40
  1015.9 8.4 copy-start.37
  (39 other events, 117.2 us)
Sparse Core Ops, SparseCore 0:
  9.6 19.4 all-gather.9
  30.6 25.3 all-gather.13
  58.7 49.3 all-gather.11
  109.5 21.0 all-gather.15
  132.0 43.3 all-gather.17
  176.9 43.3 all-gather.19
  221.9 43.3 all-gather.21
  322.7 167.4 reduce-scatter.9
  492.7 20.6 reduce-scatter.15
  515.9 21.6 reduce-scatter.17
  540.7 31.4 reduce-scatter.11
  575.3 31.4 reduce-scatter.19
  609.9 24.8 reduce-scatter.13
  637.4 54.8 reduce-scatter.21
  694.7 54.8 reduce-scatter.23
  752.1 54.8 reduce-scatter.25
  811.5 204.3 all-reduce.6
where the time goes:
time: 1050 us; the launch traced here: 1040 us
  waiting for transfers between devices  789 us (75%)
  matrix products  94.2 us (9%)
  blocking collectives  57.4 us (5%)
  local copies, waits for them, and re-layouts  45.5 us (4%)
  other arithmetic  33 us (3%)
  between operations  16 us (2%)
    psum x1, waiting for transfers between devices, on_device(): lax.psum(shards[1].astype(jnp.bfloat16), 'ctx').astype(jnp.float32)  168 us
    reduce_scatter x1, waiting for transfers between devices, on_device(): lax.psum_scatter(lax.dynamic_slice_in_dim(padded, offset, row_count, 0).a...  153 us
    reduce_scatter x1, waiting for transfers between devices, on_device(): lax.psum_scatter(gate_w_grad.astype(jnp.bfloat16), 'fsdp', scatter_dimens...  57.5 us
    reduce_scatter x1, waiting for transfers between devices, on_device(): lax.psum_scatter(down_grad.astype(jnp.bfloat16), 'fsdp', scatter_dimensio...  57.5 us
    reduce_scatter x1, waiting for transfers between devices, on_device(): lax.psum_scatter(up_w_grad.astype(jnp.bfloat16), 'fsdp', scatter_dimensio...  57.3 us
    all_gather x1, waiting for transfers between devices, on_device(): group_latent = lax.all_gather(latent, 'ctx', axis=0, tiled=True)  42.2 us
    all_gather x1, waiting for transfers between devices, on_device(): lax.all_gather(w_down, 'fsdp', axis=0, tiled=True)  39.1 us
    all_gather x1, waiting for transfers between devices, on_device(): lax.all_gather(w_up, 'fsdp', axis=1, tiled=True)  38.9 us
  transfers between devices with their start and end apart: 17, of which 15 were waited for; matrix products, arithmetic and copies ran while one was open for 9% of the time, Pallas kernels for 0%

commit v1 on v0

--- a/solution.py
+++ b/solution.py
@@ -10,6 +10,24 @@
 SEQ_MAX = 4096
 EPS = 1e-06
 NEGATIVE = -1e30
+
+
+def ring_gather(shard, axis, dim):
+    ways, here, step = (lax.axis_size(axis), lax.axis_index(axis), shard.shape[dim])
+    shape = [n * ways if d == dim else n for d, n in enumerate(shard.shape)]
+    full = lax.dynamic_update_slice_in_dim(
+        jnp.zeros(shape, shard.dtype), shard, here * step, axis=dim
+    )
+    going_up = going_down = shard
+    for far in range(1, ways // 2 + 1):
+        going_up = lax.ppermute(going_up, axis, [(d, (d + 1) % ways) for d in range(ways)])
+        full = lax.dynamic_update_slice_in_dim(full, going_up, (here - far) % ways * step, axis=dim)
+        if 2 * far < ways:
+            going_down = lax.ppermute(going_down, axis, [(d, (d - 1) % ways) for d in range(ways)])
+            full = lax.dynamic_update_slice_in_dim(
+                full, going_down, (here + far) % ways * step, axis=dim
+            )
+    return full
 
 
 def norm_scale(values):
@@ -81,7 +99,7 @@
     gain_two, gate_full, up_full, down_full = (
         lax.all_gather(norm2_gain, "fsdp", axis=0, tiled=True),
         lax.all_gather(w_gate, "fsdp", axis=1, tiled=True),
-        lax.all_gather(w_up, "fsdp", axis=1, tiled=True),
+        ring_gather(w_up, "fsdp", 1),
         lax.all_gather(w_down, "fsdp", axis=0, tiled=True),
     )
     gain_one_f = gain_one.astype(jnp.float32)

time: 1050 us -> 1000 us (0.952)
  waiting for transfers between devices: 789 us -> 729 us
  local copies, waits for them, and re-layouts: 45.5 us -> 61.2 us
  matrix products: 94.2 us -> 82.3 us
    ppermute x0 -> x3, waiting for transfers between devices: none -> 42.9 us  [the longest x2 42.9 us: ring_gather(): lax.ppermute(going_up, axis, [(d, (d + 1) % ways) for d in range(ways)])]
    all_gather x1, waiting for transfers between devices: 42.2 us -> 0.02 us  [on_device(): group_latent = lax.all_gather(latent, 'ctx', axis=0, tiled=True)]
    all_gather x1 -> x0, waiting for transfers between devices: 38.9 us -> none  [on_device(): lax.all_gather(w_up, 'fsdp', axis=1, tiled=True)]
    reduce_scatter x1, waiting for transfers between devices: 2.6 us -> 24.9 us  [on_device(): lax.psum_scatter(key_up_grad.astype(jnp.bfloat16), 'fsdp', scatter_dimens...]
    reduce_scatter x1, waiting for transfers between devices: 24.2 us -> 5.11 us  [on_device(): lax.psum_scatter(value_grad.astype(jnp.bfloat16), 'fsdp', scatter_dimensi...]
    all_gather x1, waiting for transfers between devices: 36.1 us -> 19.8 us  [on_device(): lax.all_gather(w_gate, 'fsdp', axis=1, tiled=True)]
    all_gather x1, blocking collectives: 5.07 us -> 18.8 us  [on_device(): lax.all_gather(norm2_gain, 'fsdp', axis=0, tiled=True)]
  transfers between devices with their start and end apart: 17 -> 19, of which waited for: 15 -> 14; matrix products, arithmetic and copies ran while one was open for 9% -> 10% of each run, Pallas kernels for 0% -> 0%
where the time goes in v1:
time: 1000 us; the launch traced here: 990 us
  waiting for transfers between devices  729 us (73%)
  matrix products  82.3 us (8%)
  blocking collectives  67.7 us (7%)
  local copies, waits for them, and re-layouts  61.2 us (6%)
  other arithmetic  30.6 us (3%)
  between operations  16 us (2%)
    psum x1, waiting for transfers between devices, on_device(): lax.psum(shards[1].astype(jnp.bfloat16), 'ctx').astype(jnp.float32)  168 us
    reduce_scatter x1, waiting for transfers between devices, on_device(): lax.psum_scatter(lax.dynamic_slice_in_dim(padded, offset, row_count, 0).a...  145 us
    reduce_scatter x1, waiting for transfers between devices, on_device(): lax.psum_scatter(gate_w_grad.astype(jnp.bfloat16), 'fsdp', scatter_dimens...  57.6 us
    reduce_scatter x1, waiting for transfers between devices, on_device(): lax.psum_scatter(down_grad.astype(jnp.bfloat16), 'fsdp', scatter_dimensio...  57.4 us
    reduce_scatter x1, waiting for transfers between devices, on_device(): lax.psum_scatter(up_w_grad.astype(jnp.bfloat16), 'fsdp', scatter_dimensio...  57.3 us
    ppermute x2, waiting for transfers between devices, ring_gather(): lax.ppermute(going_up, axis, [(d, (d + 1) % ways) for d in range(ways)])  42.9 us
    all_gather x1, waiting for transfers between devices, on_device(): lax.all_gather(w_down, 'fsdp', axis=0, tiled=True)  38.9 us
    reduce_scatter x1, waiting for transfers between devices, on_device(): lax.psum_scatter(query_w_grad.astype(jnp.bfloat16), 'fsdp', scatter_dimen...  34.7 us
  transfers between devices with their start and end apart: 19, of which 14 were waited for; matrix products, arithmetic and copies ran while one was open for 10% of the time, Pallas kernels for 0%

profile of v1, /device:TPU:0, one launch (start us, length us, event | category | flops | bytes accessed | tf_op | source)
XLA Modules:
  0.0 990.1 jit_solution(9024557704117578664)
XLA Ops:
  16.6 12.4 %all-gather.9.cloned.1.call-done = bf16[1024,512]{1,0:T(8,128)(2,1)} async-done(((bf16[256,512]{1,0:T(8,128)(2,1)}), bf16[1024,512]{1,0:T(8,128)(2,1)}) %all-gather.9.cloned.1.call-update) | async-done | bytes 1048592 | tf_op jit(solution)/shard_map/all_gather | solution.py:94
  35.3 42.9 %collective-permute-done = bf16[1024,704]{0,1:T(8,128)(2,1)} collective-permute-done((bf16[1024,704]{0,1:T(8,128)(2,1)S(1)}, bf16[1024,704]{0,1:T(8,128)(2,1)}, u32[]{:S(2)}, u32[]{:S(2)}) %collective-permute-start) | collective-permute-done | bytes 1441824 | tf_op jit(solution)/shard_map/ppermute | solution.py:23
  78.9 18.8 %all-gather.1 = bf16[4,1,256]{2,1,0:T(2,128)(2,1)S(1)} all-gather(bf16[1,1,256]{2,1,0:T(2,128)(2,1)S(1)} %reshape.281), channel_id=1, replica_groups=mesh['ctx'=8,'fsdp'=4] {'fsdp'}, dimensions={0}, use_global_device_ids=true | all-gather | bytes 2560 | tf_op jit(solution)/shard_map/all_gather | solution.py:100
  102.2 7.0 all_gather.34
  109.3 7.7 all_gather.35
  138.9 10.8 %while.41 = (s32[]{:T(128)}, f32[2,8,256]{2,1,0:T(8,128)S(1)}, f32[2,8,256]{2,1,0:T(8,128)S(1)}, f32[2,8,256,256]{3,2,1,0:T(8,128)}, s32[]{:T(128)}, /*index=5*/...) while((s32[]{:T(128)}, f32[2,8,256]{2,1,0:T(8,128)S(1)}, ...), condition=%wide.region_6.7_spmd.clone, body=%wide.region_1.0_spmd.clone.sunk | while | flops 1089676544 | bytes 58203592 | solution.py:165
  138.9 10.4 %conditional.6 = ((f32[2,8,256]{2,1,0:T(8,128)S(1)}, f32[2,8,256]{2,1,0:T(8,128)S(1)}, f32[2,8,256,256]{3,2,1,0:T(8,128)})) conditional(s32[]{:T(128)} %convert_element_type.378, (f32[2,8,256]{2,1,0:T(8,128)S(1)}, f32[2,8,256]{2,1,0:T(8,128)S(1)}, f32[2,8,256,256]{3,2,1,0:T(8,128)}) %tuple.129, (s32[]{:T(128)}, s32[]{:T(128)}, s32[]{:T(128)}, ...), branch_computations={%region_2.2_spmd, %region_3.5_spmd} | conditional | flops 1089676544 | bytes 58202268 | solution.py:146
  149.7 6.2 copy.71
  164.2 19.8 %all-gather.17.cloned.1.call-done = bf16[1024,2816]{0,1:T(8,128)(2,1)} async-done(((bf16[1024,704]{0,1:T(8,128)(2,1)}), bf16[1024,2816]{0,1:T(8,128)(2,1)}) %all-gather.17.cloned.1.call-update) | async-done | bytes 5767184 | tf_op jit(solution)/shard_map/all_gather | solution.py:101
  189.9 38.9 %all-gather.19.cloned.1.call-done = bf16[2816,1024]{1,0:T(8,128)(2,1)} async-done(((bf16[704,1024]{1,0:T(8,128)(2,1)}), bf16[2816,1024]{1,0:T(8,128)(2,1)}) %all-gather.19.cloned.1.call-update) | async-done | bytes 5767184 | tf_op jit(solution)/shard_map/all_gather | solution.py:103
  233.5 6.6 multiply_convert_fusion
  262.1 17.3 %while.42 = (s32[]{:T(128)}, f32[2,8,256,256]{3,2,1,0:T(8,128)}, bf16[2048,512]{0,1:T(8,128)(2,1)}, s32[]{:T(128)}, s32[]{:T(128)}, /*index=5*/s32[]{:T(128)}, s...) while((s32[]{:T(128)}, f32[2,8,256,256]{3,2,1,0:T(8,128)}, ...), condition=%wide.region_13.14_spmd.clone, body=%wide.region_10.13_spmd.clone.sunk | while | flops 2699625728 | bytes 80993792 | solution.py:264
  262.1 11.2 %conditional.7 = (f32[2,8,256,256]{3,2,1,0:T(8,128)}, bf16[256,512]{0,1:T(8,128)(2,1)S(1)}) conditional(s32[]{:T(128)} %convert_element_type.379, f32[2,8,256,256]{3,2,1,0:T(8,128)} %get-tuple-element.1157, (s32[]{:T(128)}, s32[]{:T(128)}, s32[]{:T(128)}, s32[]{:T(128)}, bf16[2048,512]{0,1:T(8,128)(2,1)}, ...), branch_computations={%region_11.11_spmd, %region_12.12_spmd} | conditional | flops 2699625728 | bytes 80468128 | solution.py:251
  300.5 144.5 %reduce-scatter.10.cloned.1.call-done = bf16[256,512]{0,1:T(8,128)(2,1)} async-done(((bf16[2048,512]{0,1:T(8,128)(2,1)}), bf16[256,512]{0,1:T(8,128)(2,1)}) %reduce-scatter.10.cloned.1.call-update) | async-done | bytes 262160 | tf_op jit(solution)/shard_map/reduce_scatter | solution.py:269
  468.2 24.9 %reduce-scatter.16.cloned.1.call-done = bf16[256,256]{1,0:T(8,128)(2,1)} async-done(((bf16[1024,256]{1,0:T(8,128)(2,1)}), bf16[256,256]{1,0:T(8,128)(2,1)}) %reduce-scatter.16.cloned.1.call-update) | async-done | bytes 131088 | tf_op jit(solution)/shard_map/reduce_scatter | solution.py:304
  493.1 34.4 %reduce-scatter.20.cloned.1.call-done = bf16[256,1024]{1,0:T(8,128)(2,1)} async-done(((bf16[1024,1024]{1,0:T(8,128)(2,1)}), bf16[256,1024]{1,0:T(8,128)(2,1)}) %reduce-scatter.20.cloned.1.call-update) | async-done | bytes 524304 | tf_op jit(solution)/shard_map/reduce_scatter | solution.py:310
  527.5 34.7 %reduce-scatter.12.cloned.1.call-done = bf16[256,1024]{1,0:T(8,128)(2,1)} async-done(((bf16[1024,1024]{1,0:T(8,128)(2,1)}), bf16[256,1024]{1,0:T(8,128)(2,1)}) %reduce-scatter.12.cloned.1.call-update) | async-done | bytes 524304 | tf_op jit(solution)/shard_map/reduce_scatter | solution.py:298
  562.2 27.9 %reduce-scatter.14.cloned.1.call-done = bf16[256,512]{1,0:T(8,128)(2,1)} async-done(((bf16[1024,512]{1,0:T(8,128)(2,1)}), bf16[256,512]{1,0:T(8,128)(2,1)}) %reduce-scatter.14.cloned.1.call-update) | async-done | bytes 262160 | tf_op jit(solution)/shard_map/reduce_scatter | solution.py:301
  590.1 57.6 %reduce-scatter.22.cloned.1.call-done = bf16[1024,704]{0,1:T(8,128)(2,1)} async-done(((bf16[1024,2816]{0,1:T(8,128)(2,1)}), bf16[1024,704]{0,1:T(8,128)(2,1)}) %reduce-scatter.22.cloned.1.call-update) | async-done | bytes 1441808 | tf_op jit(solution)/shard_map/reduce_scatter | solution.py:316
  647.7 57.3 %reduce-scatter.24.cloned.1.call-done = bf16[1024,704]{0,1:T(8,128)(2,1)} async-done(((bf16[1024,2816]{0,1:T(8,128)(2,1)}), bf16[1024,704]{0,1:T(8,128)(2,1)}) %reduce-scatter.24.cloned.1.call-update) | async-done | bytes 1441808 | tf_op jit(solution)/shard_map/reduce_scatter | solution.py:319
  705.0 57.4 %reduce-scatter.26.cloned.1.call-done = bf16[704,1024]{1,0:T(8,128)(2,1)} async-done(((bf16[2816,1024]{1,0:T(8,128)(2,1)}), bf16[704,1024]{1,0:T(8,128)(2,1)}) %reduce-scatter.26.cloned.1.call-update) | async-done | bytes 1441808 | tf_op jit(solution)/shard_map/reduce_scatter | solution.py:322
  773.1 6.1 all-reduce.4
  779.3 22.1 %all-reduce.2 = (bf16[256]{0:T(256)(128)(2,1)S(1)}, bf16[256]{0:T(256)(128)(2,1)S(1)}) all-reduce(bf16[256]{0:T(256)(128)(2,1)S(1)} %dynamic-slice.1, bf16[256]{0:T(256)(128)(2,1)S(1)} %dynamic-slice.3), channel_id=1, replica_groups=mesh['ctx'=8,'fsdp'=4] {'ctx'}, use_global_device_ids=true, to_apply=%region_18.19 | all-reduce | flops 512 | bytes 2048 | tf_op jit(solution)/shard_map/psum | solution.py:327
  803.8 167.7 %all-reduce.7.cloned.1.call-done = (bf16[256,1024]{1,0:T(8,128)(2,1)}, bf16[256,512]{1,0:T(8,128)(2,1)}, bf16[256,256]{1,0:T(8,128)(2,1)}, bf16[256,256]{1,0:T(8...) async-done(((bf16[256,1024]{1,0:T(8,128)(2,1)}, bf16[256,512]{1,0:T(8,128)(2,1)}, ...) | async-done | bytes 5898256 | tf_op jit(solution)/shard_map/psum | solution.py:328
  (278 shorter events, 178.5 us)
Async XLA Ops:
  7.2 21.8 %all-gather.9.cloned.1.call-start = ((), (), s32[]{:S(2)}) async-start(), calls=%async_computation.9 | async-start | bytes 1310720 | tf_op jit(solution)/shard_map/all_gather | solution.py:94
  7.9 117.0 %all-gather.13.cloned.1.call-start = ((), (), s32[]{:S(2)}) async-start(), calls=%async_computation.11 | async-start | bytes 2621440 | tf_op jit(solution)/shard_map/all_gather | solution.py:93
  8.7 123.8 %all-gather.11.cloned.1.call-start = ((), (), s32[]{:S(2)}) async-start(), calls=%async_computation.10 | async-start | bytes 2359296 | tf_op jit(solution)/shard_map/all_gather | solution.py:158
  15.3 109.6 %copy-start.42 = (f32[4,1,256]{2,1,0:T(1,128)}, f32[4,1,256]{2,1,0:T(1,128)S(1)}, u32[]{:S(2)}) copy-start(f32[4,1,256]{2,1,0:T(1,128)S(1)} %convert_element_type.282) | copy-start | bytes 12292
  16.6 108.3 %copy-start.44 = (f32[256]{0:T(256)}, f32[256]{0:T(256)S(1)}, u32[]{:S(2)}) copy-start(f32[256]{0:T(256)S(1)} %add_rsqrt_fusion.1) | copy-start | bytes 3076
  29.0 49.9 %copy-start.46 = (bf16[256]{0:T(256)(128)(2,1)S(1)}, bf16[256]{0:T(256)(128)(2,1)}, u32[]{:S(2)}) copy-start(bf16[256]{0:T(256)(128)(2,1)} %param.30) | copy-start | bytes 1540
  31.7 128.7 %all-gather.15.cloned.1.call-start = ((), (), s32[]{:S(2)}) async-start(), calls=%async_computation.12 | async-start | bytes 2621440 | tf_op jit(solution)/shard_map/all_gather | solution.py:97
  32.3 151.6 %all-gather.17.cloned.1.call-start = ((), (), s32[]{:S(2)}) async-start(), calls=%async_computation.13 | async-start | bytes 7208960 | tf_op jit(solution)/shard_map/all_gather | solution.py:101
  32.9 195.9 %all-gather.19.cloned.1.call-start = ((), (), s32[]{:S(2)}) async-start(), calls=%async_computation.14 | async-start | bytes 7208960 | tf_op jit(solution)/shard_map/all_gather | solution.py:103
  33.5 411.5 %reduce-scatter.10.cloned.1.call-start = ((), (), s32[]{:S(2)}) async-start(), calls=%async_computation.15 | async-start | bytes 2359296 | tf_op jit(solution)/shard_map/reduce_scatter | solution.py:269
  33.5 44.7 %collective-permute-start = (bf16[1024,704]{0,1:T(8,128)(2,1)S(1)}, bf16[1024,704]{0,1:T(8,128)(2,1)}, u32[]{:S(2)}, u32[]{:S(2)}) collective-permute-start(bf16[1024,704]{0,1:T(8,128)(2,1)S(1)} %copy-done.30), channel_id=1, source_target_pairs={{0,1},{1,2},{2,3},{3,0},{4,5},{5,6},{6,7},{7,4},{8,9},{9,10},{10,1... | collective-permute-start | bytes 4325384 | tf_op jit(solution)/shard_map/ppermute | solution.py:23
  33.8 85.8 %collective-permute-start.1 = (bf16[1024,704]{0,1:T(8,128)(2,1)S(1)}, bf16[1024,704]{0,1:T(8,128)(2,1)}, u32[]{:S(2)}, u32[]{:S(2)}) collective-permute-start(bf16[1024,704]{0,1:T(8,128)(2,1)S(1)} %copy-done.30), channel_id=1, source_target_pairs={{0,3},{1,0},{2,1},{3,2},{4,7},{5,4},{6,5},{7,6},{8,11},{9,8},{10,9... | collective-permute-start | bytes 4325384 | tf_op jit(solution)/shard_map/ppermute | solution.py:26
  78.2 44.0 %collective-permute-start.2 = (bf16[1024,704]{0,1:T(8,128)(2,1)}, bf16[1024,704]{0,1:T(8,128)(2,1)}, u32[]{:S(2)}, u32[]{:S(2)}) collective-permute-start(bf16[1024,704]{0,1:T(8,128)(2,1)} %collective-permute-done), channel_id=1, source_target_pairs={{0,1},{1,2},{2,3},{3,0},{4,5},{5,6},{6,7},{7,4},{8,9},{9,10},{10,1... | collective-permute-start | bytes 4325384 | tf_op jit(solution)/shard_map/ppermute | solution.py:23
  285.3 182.9 %reduce-scatter.18.cloned.1.call-start = ((), (), s32[]{:S(2)}) async-start(), calls=%async_computation.19 | async-start | bytes 655360 | tf_op jit(solution)/shard_map/reduce_scatter | solution.py:307
  288.0 205.1 %reduce-scatter.16.cloned.1.call-start = ((), (), s32[]{:S(2)}) async-start(), calls=%async_computation.18 | async-start | bytes 655360 | tf_op jit(solution)/shard_map/reduce_scatter | solution.py:304
  291.8 235.7 %reduce-scatter.20.cloned.1.call-start = ((), (), s32[]{:S(2)}) async-start(), calls=%async_computation.20 | async-start | bytes 2621440 | tf_op jit(solution)/shard_map/reduce_scatter | solution.py:310
  295.3 266.9 %reduce-scatter.12.cloned.1.call-start = ((), (), s32[]{:S(2)}) async-start(), calls=%async_computation.16 | async-start | bytes 2621440 | tf_op jit(solution)/shard_map/reduce_scatter | solution.py:298
  300.4 147.2 %copy-start.29 = (bf16[256,2816]{1,0:T(8,128)(2,1)S(1)}, bf16[256,2816]{1,0:T(8,128)(2,1)}, u32[]{:S(2)}) copy-start(bf16[256,2816]{1,0:T(8,128)(2,1)} %copy-done.28) | copy-start | bytes 4325380
  300.4 289.7 %reduce-scatter.14.cloned.1.call-start = ((), (), s32[]{:S(2)}) async-start(), calls=%async_computation.17 | async-start | bytes 1310720 | tf_op jit(solution)/shard_map/reduce_scatter | solution.py:301
  447.5 200.2 %reduce-scatter.22.cloned.1.call-start = ((), (), s32[]{:S(2)}) async-start(), calls=%async_computation.21 | async-start | bytes 7208960 | tf_op jit(solution)/shard_map/reduce_scatter | solution.py:316
  451.8 253.2 %reduce-scatter.24.cloned.1.call-start = ((), (), s32[]{:S(2)}) async-start(), calls=%async_computation.22 | async-start | bytes 7208960 | tf_op jit(solution)/shard_map/reduce_scatter | solution.py:319
  457.3 305.2 %reduce-scatter.26.cloned.1.call-start = ((), (), s32[]{:S(2)}) async-start(), calls=%async_computation.23 | async-start | bytes 7208960 | tf_op jit(solution)/shard_map/reduce_scatter | solution.py:322
  463.0 508.5 %all-reduce.7.cloned.1.call-start = ((), (), s32[]{:S(2)}) async-start(), calls=%async_computation.24 | async-start | bytes 11796480 | tf_op jit(solution)/shard_map/psum | solution.py:328
  772.4 30.2 %copy-start.8 = (f32[256,1024]{1,0:T(8,128)S(1)}, f32[256,1024]{1,0:T(8,128)}, u32[]{:S(2)}) copy-start(f32[256,1024]{1,0:T(8,128)} %copy-done.7) | copy-start | bytes 3145732
  (46 other events, 156.7 us)
Sparse Core Ops, SparseCore 0:
  9.6 19.4 all-gather.8
  30.6 33.9 all-gather.12
  67.3 49.2 all-gather.10
  118.0 21.0 all-gather.14
  140.5 43.3 all-gather.16
  185.4 43.3 all-gather.18
  285.4 159.5 reduce-scatter.9
  447.5 20.6 reduce-scatter.17
  471.4 21.6 reduce-scatter.15
  496.0 31.4 reduce-scatter.19
  530.8 31.4 reduce-scatter.11
  565.2 24.8 reduce-scatter.13
  592.8 54.8 reduce-scatter.21
  650.1 54.8 reduce-scatter.23
  707.5 54.8 reduce-scatter.25
  766.9 204.5 all-reduce.6
